TPU v7x, 128 devices: a whole 4x4x4 slice. The times are simulated.
128 devices in a mesh: row: 16 (over x, y), col: 4 (over z), layer: 2 (over core).
Axes of the slice: x: 4, y: 4, z: 4, core: 2. Of those that a mesh axis runs over, the one named last changes fastest.
Arguments:
- density: float32 [4096, 4096], P('row', ('col', 'layer')), may hold values from -2 to 2
- masks: int32 [6, 64, 64], replicated, may hold values from 0 to 1, as said below
- branch: int32 [5], replicated, may hold values from 0 to 1, as said below
- perm: int32 [64], replicated, may hold values from 0 to 63, each once
Outputs:
- purified: float32 [4096, 4096], P('row', ('col', 'layer'))
Inputs may be any that keep to these rules, and one draw needn't show every extreme that they name: masks are symmetric in their last two dimensions, every diagonal block is occupied, and block (i, j) of masks[s] is occupied only where the cyclic distance between i and j is at most 6 + s. `branch`: both values occur among the steps. `perm`: a permutation of 0..63.
All inputs are finite; a program needn't handle non-finite values.
Results may differ from a plain program's by a relative error of at most 0.0003.
Values sent between devices are 32-bit elements; how exact they have to be, the bound alone decides.
No kernel may reach another device: no remote copies, remote signals or barrier semaphores. Data moves between devices by JAX's collectives and lax.ppermute only.
A program may use at most 64 MiB of HBM per device.

v0:
```python
import jax
import jax.numpy as jnp
from jax import lax
from jax.sharding import PartitionSpec as P

BS = 64
STEPS = 5


def expand(block_mask):
    grown = jnp.repeat(block_mask, BS, axis=0)
    return jnp.repeat(grown, BS, axis=1).astype(jnp.float32)


def shards(density, masks, branch, perm):
    rows_here = density.shape[0]
    cols_here = density.shape[1]
    row_blocks = rows_here // BS
    col_blocks = cols_here // BS
    row_start = lax.axis_index("row") * row_blocks
    col_start = lax.axis_index(("col", "layer")) * col_blocks
    row_ids = lax.dynamic_slice_in_dim(perm, row_start, row_blocks)
    col_ids = lax.dynamic_slice_in_dim(perm, col_start, col_blocks)
    local_masks = jnp.take(jnp.take(masks, row_ids, axis=1), col_ids, axis=2)
    current = density * expand(local_masks[0])
    for step in range(STEPS):
        panel = lax.all_gather(current, ("col", "layer"), axis=1, tiled=True)
        square = jnp.dot(
            panel,
            lax.all_gather(current, "row", axis=0, tiled=True),
            preferred_element_type=jnp.float32,
            precision=lax.Precision.HIGHEST,
        )
        picked = jnp.where(branch[step] == 1, 2.0 * current - square, square)
        current = picked * expand(local_masks[step + 1])
    return current


def solution(mesh):
    return jax.shard_map(
        shards,
        mesh=mesh,
        in_specs=(P("row", ("col", "layer")), P(), P(), P()),
        out_specs=P("row", ("col", "layer")),
        check_vma=False,
    )
```

profile of v0, /device:TPU:1, one launch (start us, length us, event | category | flops | bytes accessed | tf_op | source)
XLA Modules:
  0.0 603.6 jit_solution(2125554987655784131)
XLA Ops:
  6.5 0.8 compare_and_fusion
  7.3 0.2 copy-done
  7.5 0.6 gather_fusion
  8.1 0.1 select_bitcast_fusion.1
  8.1 0.1 copy.24
  8.3 0.7 compare_and_fusion.1
  9.0 0.6 gather_fusion.1
  9.6 0.1 copy.25
  9.7 0.1 copy.26
  9.8 0.1 broadcast_in_dim.66
  9.9 0.1 convert_element_type.86
  10.0 0.2 copy.27
  10.2 1.9 mul.45
  12.1 0.0 all-gather.11.cloned.1.call-update
  12.2 0.0 all-gather.13.cloned.1.call-start
  12.2 0.7 all-gather.13.cloned.1.call-update
  12.9 0.0 all-gather.15.cloned.1.call-start
  13.0 0.1 copy.28
  13.0 0.1 broadcast_in_dim.68
  13.1 0.1 convert_element_type.90
  13.3 0.2 copy.29
  13.5 1.5 fusion.11
  15.5 32.8 %all-gather.11.cloned.1.call-done = f32[256,4096]{1,0:T(8,128)} async-done(((f32[256,512]{1,0:T(8,128)}), f32[256,4096]{1,0:T(8,128)}) %all-gather.11.cloned.1.call-update) | async-done | bytes 4194320 | tf_op jit(solution)/shard_map/all_gather | solution.py:27
  48.3 72.2 %all-gather.13.cloned.1.call-done = f32[4096,512]{1,0:T(8,128)} async-done(((f32[256,512]{1,0:T(8,128)}), f32[4096,512]{1,0:T(8,128)}) %all-gather.13.cloned.1.call-update) | async-done | bytes 8388624 | tf_op jit(solution)/shard_map/all_gather | solution.py:30
  120.5 11.5 %fusion = f32[256,512]{1,0:T(8,128)} fusion(f32[256,512]{1,0:T(8,128)S(1)} %copy.29, f32[256,512]{1,0:T(8,128)} %mul.45, pred[]{:T(512)} %bitcast.4, f32[256,4096]{1,0:T(8,128)} %all-gather.11.cloned.1.call-done, f32[4096,512]{1,0:T(8,128)} %all-gather.13.cloned.1.call-done), kind=kOutput, calls=%fused_computation.7 | convolution fusion | flops 6442975232 | bytes 14155777 | tf_op jit(solution)/shard_map/dot_general | solution.py:28
  132.0 0.0 all-gather.17.cloned.1.call-start
  132.0 0.5 all-gather.17.cloned.1.call-update
  132.6 0.0 all-gather.19.cloned.1.call-start
  132.6 0.1 copy.30
  132.7 0.1 broadcast_in_dim.70
  132.8 0.1 convert_element_type.94
  132.9 0.2 copy.31
  133.8 30.8 %all-gather.15.cloned.1.call-done = f32[256,4096]{1,0:T(8,128)} async-done(((f32[256,512]{1,0:T(8,128)}), f32[256,4096]{1,0:T(8,128)}) %all-gather.15.cloned.1.call-update) | async-done | bytes 4194320 | tf_op jit(solution)/shard_map/all_gather | solution.py:27
  164.6 72.0 %all-gather.17.cloned.1.call-done = f32[4096,512]{1,0:T(8,128)} async-done(((f32[256,512]{1,0:T(8,128)}), f32[4096,512]{1,0:T(8,128)}) %all-gather.17.cloned.1.call-update) | async-done | bytes 8388624 | tf_op jit(solution)/shard_map/all_gather | solution.py:30
  236.6 11.5 %fusion.1 = f32[256,512]{1,0:T(8,128)} fusion(f32[256,512]{1,0:T(8,128)S(1)} %copy.31, f32[256,512]{1,0:T(8,128)} %fusion, pred[]{:T(512)} %bitcast.3, f32[256,4096]{1,0:T(8,128)} %all-gather.15.cloned.1.call-done, f32[4096,512]{1,0:T(8,128)} %all-gather.17.cloned.1.call-done), kind=kOutput, calls=%fused_computation.8 | convolution fusion | flops 6442975232 | bytes 14155777 | tf_op jit(solution)/shard_map/dot_general | solution.py:28
  248.1 0.0 all-gather.21.cloned.1.call-start
  248.2 0.5 all-gather.21.cloned.1.call-update
  248.7 0.2 all-gather.23.cloned.1.call-start
  248.9 0.1 copy.32
  249.0 0.1 broadcast_in_dim.72
  249.1 0.1 convert_element_type.98
  249.2 0.2 copy.33
  250.1 30.7 %all-gather.19.cloned.1.call-done = f32[256,4096]{1,0:T(8,128)} async-done(((f32[256,512]{1,0:T(8,128)}), f32[256,4096]{1,0:T(8,128)}) %all-gather.19.cloned.1.call-update) | async-done | bytes 4194320 | tf_op jit(solution)/shard_map/all_gather | solution.py:27
  280.8 72.0 %all-gather.21.cloned.1.call-done = f32[4096,512]{1,0:T(8,128)} async-done(((f32[256,512]{1,0:T(8,128)}), f32[4096,512]{1,0:T(8,128)}) %all-gather.21.cloned.1.call-update) | async-done | bytes 8388624 | tf_op jit(solution)/shard_map/all_gather | solution.py:30
  352.8 11.5 %fusion.2 = f32[256,512]{1,0:T(8,128)} fusion(f32[256,512]{1,0:T(8,128)S(1)} %copy.33, f32[256,512]{1,0:T(8,128)} %fusion.1, pred[]{:T(512)} %bitcast.2, f32[256,4096]{1,0:T(8,128)} %all-gather.19.cloned.1.call-done, f32[4096,512]{1,0:T(8,128)} %all-gather.21.cloned.1.call-done), kind=kOutput, calls=%fused_computation.9 | convolution fusion | flops 6442975232 | bytes 14155777 | tf_op jit(solution)/shard_map/dot_general | solution.py:28
  364.3 0.0 all-gather.25.cloned.1.call-start
  364.4 0.7 all-gather.25.cloned.1.call-update
  365.1 0.0 all-gather.27.cloned.1.call-start
  365.1 0.1 copy.34
  365.2 0.1 broadcast_in_dim.74
  365.3 0.1 convert_element_type.102
  365.4 0.2 copy.35
  366.2 30.7 %all-gather.23.cloned.1.call-done = f32[256,4096]{1,0:T(8,128)} async-done(((f32[256,512]{1,0:T(8,128)}), f32[256,4096]{1,0:T(8,128)}) %all-gather.23.cloned.1.call-update) | async-done | bytes 4194320 | tf_op jit(solution)/shard_map/all_gather | solution.py:27
  397.0 72.2 %all-gather.25.cloned.1.call-done = f32[4096,512]{1,0:T(8,128)} async-done(((f32[256,512]{1,0:T(8,128)}), f32[4096,512]{1,0:T(8,128)}) %all-gather.25.cloned.1.call-update) | async-done | bytes 8388624 | tf_op jit(solution)/shard_map/all_gather | solution.py:30
  469.1 11.5 %fusion.3 = f32[256,512]{1,0:T(8,128)} fusion(f32[256,512]{1,0:T(8,128)S(1)} %copy.35, f32[256,512]{1,0:T(8,128)} %fusion.2, pred[]{:T(512)} %bitcast.1, f32[256,4096]{1,0:T(8,128)} %all-gather.23.cloned.1.call-done, f32[4096,512]{1,0:T(8,128)} %all-gather.25.cloned.1.call-done), kind=kOutput, calls=%fused_computation.10 | convolution fusion | flops 6442975232 | bytes 14155777 | tf_op jit(solution)/shard_map/dot_general | solution.py:28
  480.6 0.3 all-gather.29.cloned.1.call-start
  480.9 0.3 all-gather.29.cloned.1.call-update
  481.2 0.1 copy.36
  481.3 0.1 broadcast_in_dim.76
  481.4 0.1 convert_element_type.106
  481.5 0.2 copy.37
  482.4 30.8 %all-gather.27.cloned.1.call-done = f32[256,4096]{1,0:T(8,128)} async-done(((f32[256,512]{1,0:T(8,128)}), f32[256,4096]{1,0:T(8,128)}) %all-gather.27.cloned.1.call-update) | async-done | bytes 4194320 | tf_op jit(solution)/shard_map/all_gather | solution.py:27
  513.2 72.0 %all-gather.29.cloned.1.call-done = f32[4096,512]{1,0:T(8,128)} async-done(((f32[256,512]{1,0:T(8,128)}), f32[4096,512]{1,0:T(8,128)}) %all-gather.29.cloned.1.call-update) | async-done | bytes 8388624 | tf_op jit(solution)/shard_map/all_gather | solution.py:30
  585.3 11.5 %fusion.4 = f32[256,512]{1,0:T(8,128)} fusion(f32[256,512]{1,0:T(8,128)S(1)} %copy.37, f32[256,512]{1,0:T(8,128)} %fusion.3, pred[]{:T(512)} %bitcast, f32[256,4096]{1,0:T(8,128)} %all-gather.27.cloned.1.call-done, f32[4096,512]{1,0:T(8,128)} %all-gather.29.cloned.1.call-done), kind=kOutput, calls=%fused_computation.11 | convolution fusion | flops 6442975232 | bytes 14155777 | tf_op jit(solution)/shard_map/dot_general | solution.py:28
  (18 shorter events, 0.3 us)
Async XLA Ops:
  6.5 0.9 copy-start
  6.5 41.8 %all-gather.11.cloned.1.call-start = ((), (), s32[]{:S(2)}) async-start(), calls=%async_computation | async-start | bytes 4718592 | tf_op jit(solution)/shard_map/all_gather | solution.py:27
  12.2 108.3 %all-gather.13.cloned.1.call-start = ((), (), s32[]{:S(2)}) async-start(), calls=%async_computation.1 | async-start | bytes 8912896 | tf_op jit(solution)/shard_map/all_gather | solution.py:30
  12.9 151.7 %all-gather.15.cloned.1.call-start = ((), (), s32[]{:S(2)}) async-start(), calls=%async_computation.2 | async-start | bytes 4718592 | tf_op jit(solution)/shard_map/all_gather | solution.py:27
  132.0 104.7 %all-gather.17.cloned.1.call-start = ((), (), s32[]{:S(2)}) async-start(), calls=%async_computation.3 | async-start | bytes 8912896 | tf_op jit(solution)/shard_map/all_gather | solution.py:30
  132.6 148.2 %all-gather.19.cloned.1.call-start = ((), (), s32[]{:S(2)}) async-start(), calls=%async_computation.4 | async-start | bytes 4718592 | tf_op jit(solution)/shard_map/all_gather | solution.py:27
  248.1 104.7 %all-gather.21.cloned.1.call-start = ((), (), s32[]{:S(2)}) async-start(), calls=%async_computation.5 | async-start | bytes 8912896 | tf_op jit(solution)/shard_map/all_gather | solution.py:30
  248.7 148.3 %all-gather.23.cloned.1.call-start = ((), (), s32[]{:S(2)}) async-start(), calls=%async_computation.6 | async-start | bytes 4718592 | tf_op jit(solution)/shard_map/all_gather | solution.py:27
  364.3 104.8 %all-gather.25.cloned.1.call-start = ((), (), s32[]{:S(2)}) async-start(), calls=%async_computation.7 | async-start | bytes 8912896 | tf_op jit(solution)/shard_map/all_gather | solution.py:30
  365.1 148.2 %all-gather.27.cloned.1.call-start = ((), (), s32[]{:S(2)}) async-start(), calls=%async_computation.8 | async-start | bytes 4718592 | tf_op jit(solution)/shard_map/all_gather | solution.py:27
  480.6 116.1 %copy-start.1 = (s32[6,64,64]{2,1,0:T(8,128)S(1)}, s32[6,64,64]{2,1,0:T(8,128)}, u32[]{:S(2)}) copy-start(s32[6,64,64]{2,1,0:T(8,128)} %param.5) | copy-start | bytes 294916
  480.6 104.6 %all-gather.29.cloned.1.call-start = ((), (), s32[]{:S(2)}) async-start(), calls=%async_computation.9 | async-start | bytes 8912896 | tf_op jit(solution)/shard_map/all_gather | solution.py:30
Sparse Core Ops, SparseCore 0:
  12.3 35.9 all-gather.10
  50.5 69.9 all-gather.12
  132.1 32.4 all-gather.14
  166.6 69.9 all-gather.16
  248.3 32.5 all-gather.18
  282.8 69.9 all-gather.20
  364.4 32.4 all-gather.22
  399.1 69.9 all-gather.24
  480.7 32.4 all-gather.26
  515.2 69.9 all-gather.28
where the time goes:
time: 604 us
  waiting for transfers between devices  519 us (86%)
  matrix products  57.3 us (9%)
  between operations  16.9 us (3%)
    all_gather x5, waiting for transfers between devices, shards(): lax.all_gather(current, 'row', axis=0, tiled=True)  360 us
    all_gather x5, waiting for transfers between devices, shards(): panel = lax.all_gather(current, ('col', 'layer'), axis=1, tiled=True)  156 us
    dot_general x5, matrix products, shards(): jnp.dot(panel, lax.all_gather(current, 'row', axis=0, tiled=True), prefer...  57.3 us
  transfers between devices with their start and end apart: 10, of which 10 were waited for; matrix products, arithmetic and copies ran while one was open for 1% of the time, Pallas kernels for 0%

commit v1 on v0

--- a/solution.py
+++ b/solution.py
@@ -24,7 +24,12 @@
     local_masks = jnp.take(jnp.take(masks, row_ids, axis=1), col_ids, axis=2)
     current = density * expand(local_masks[0])
     for step in range(STEPS):
-        panel = lax.all_gather(current, ("col", "layer"), axis=1, tiled=True)
+        panel = jnp.concatenate(
+            lax.all_to_all(
+                jnp.stack([current] * lax.axis_size(("col", "layer"))), ("col", "layer"), 0, 0
+            ),
+            axis=1,
+        )
         square = jnp.dot(
             panel,
             lax.all_gather(current, "row", axis=0, tiled=True),

time: 604 us -> 471 us (0.78); the launches traced: 604 us -> 463 us
  waiting for transfers between devices: 519 us -> 303 us
  matrix products: 57.3 us -> 88.5 us
  starting transfers between devices: 0.76 us -> 29.3 us
  local copies, waits for them, and re-layouts: 5.94 us -> 22.8 us
    all_gather x5, waiting for transfers between devices: 360 us -> 65.3 us  [shards(): lax.all_gather(current, 'row', axis=0, tiled=True)]
    all_to_all x0 -> x5, waiting for transfers between devices: none -> 237 us  [shards(): lax.all_to_all(jnp.stack([current] * lax.axis_size(('col', 'layer'))), ('...]
    all_gather x5 -> x0, waiting for transfers between devices: 156 us -> none  [shards(): panel = lax.all_gather(current, ('col', 'layer'), axis=1, tiled=True)]
    dot_general x5, matrix products: 57.3 us -> 88.5 us  [shards(): jnp.dot(panel, lax.all_gather(current, 'row', axis=0, tiled=True), prefer...]
    all_to_all x0 -> x5, starting transfers between devices: none -> 28.3 us  [shards(): lax.all_to_all(jnp.stack([current] * lax.axis_size(('col', 'layer'))), ('...]
    another operation x0 -> x5, local copies, waits for them, and re-layouts: none -> 11.4 us  [shards(): jnp.stack([current] * lax.axis_size(('col', 'layer')))]
    mul x0 -> x5, local copies, waits for them, and re-layouts: none -> 6.19 us  [the longest x4 4.96 us: shards(): current = picked * expand(local_masks[step + 1])]
  transfers between devices with their start and end apart: 10 -> 10, of which waited for: 10 -> 10; matrix products, arithmetic and copies ran while one was open for 1% -> 4% of each run, Pallas kernels for 0% -> 0%
where the time goes in v1:
time: 471 us; the launch traced here: 463 us
  waiting for transfers between devices  303 us (64%)
  matrix products  88.5 us (19%)
  starting transfers between devices  29.3 us (6%)
  local copies, waits for them, and re-layouts  22.8 us (5%)
  between operations  16.7 us (4%)
    all_to_all x5, waiting for transfers between devices, shards(): lax.all_to_all(jnp.stack([current] * lax.axis_size(('col', 'layer'))), ('...  237 us
    dot_general x5, matrix products, shards(): jnp.dot(panel, lax.all_gather(current, 'row', axis=0, tiled=True), prefer...  88.5 us
    all_gather x5, waiting for transfers between devices, shards(): lax.all_gather(current, 'row', axis=0, tiled=True)  65.3 us
    all_to_all x5, starting transfers between devices, shards(): lax.all_to_all(jnp.stack([current] * lax.axis_size(('col', 'layer'))), ('...  28.3 us
    another operation x5, local copies, waits for them, and re-layouts, shards(): jnp.stack([current] * lax.axis_size(('col', 'layer')))  11.4 us
  transfers between devices with their start and end apart: 10, of which 10 were waited for; matrix products, arithmetic and copies ran while one was open for 4% of the time, Pallas kernels for 0%

profile of v1, /device:TPU:1, one launch (start us, length us, event | category | flops | bytes accessed | tf_op | source)
XLA Modules:
  0.0 463.5 jit_solution(10956111079362212845)
XLA Ops:
  6.5 0.8 compare_and_fusion
  7.3 0.2 copy-done
  7.5 0.6 gather_fusion
  8.1 0.1 select_bitcast_fusion.1
  8.1 0.1 copy.29
  8.3 0.7 compare_and_fusion.1
  9.0 0.6 gather_fusion.1
  9.6 0.1 copy.30
  9.7 0.1 copy.31
  9.8 0.1 broadcast_in_dim.66
  9.9 0.1 convert_element_type.86
  10.0 0.2 copy.32
  10.2 1.9 mul.45
  12.2 1.2 copy.33
  13.4 2.3 stack.10
  15.7 6.9 %all-to-all-start = ((f32[8,256,512]{1,2,0:T(8,128)}), f32[8,256,512]{1,2,0:T(8,128)}, u32[]{:S(2)}, u32[]{:S(2)}) async-start(f32[8,256,512]{1,2,0:T(8,128)} %stack.10), calls=%async_computation | async-start | bytes 8388608 | tf_op jit(solution)/shard_map/all_to_all | solution.py:28
  22.7 0.1 copy.34
  22.7 0.1 broadcast_in_dim.68
  22.8 0.1 convert_element_type.90
  22.9 0.2 copy.35
  23.2 0.7 fusion.11
  24.4 47.1 %all-to-all-done = f32[8,256,512]{1,2,0:T(8,128)} async-done(((f32[8,256,512]{1,2,0:T(8,128)}), f32[8,256,512]{1,2,0:T(8,128)}, u32[]{:S(2)}, u32[]{:S(2)}) %all-to-all-start) | async-done | bytes 4194336 | tf_op jit(solution)/shard_map/all_to_all | solution.py:28
  71.6 14.6 %all-gather.6.cloned.1.call-done = f32[4096,512]{1,0:T(8,128)} async-done(((f32[256,512]{1,0:T(8,128)}), f32[4096,512]{1,0:T(8,128)}) %all-gather.6.cloned.1.call-update) | async-done | bytes 8388624 | tf_op jit(solution)/shard_map/all_gather | solution.py:35
  86.1 17.7 %fusion = f32[256,512]{1,0:T(8,128)} fusion(f32[256,512]{1,0:T(8,128)S(1)} %copy.35, f32[256,512]{1,0:T(8,128)S(1)} %copy-done.2, pred[]{:T(512)} %bitcast.4, f32[256,4096]{0,1:T(8,128)} %bitcast.10, f32[4096,512]{1,0:T(8,128)} %all-gather.6.cloned.1.call-done), kind=kOutput, calls=%fused_computation.7 | convolution fusion | flops 6442975232 | bytes 14155777 | tf_op jit(solution)/shard_map/dot_general | solution.py:33
  103.9 1.2 copy.36
  105.1 2.3 stack.11
  107.4 5.3 %all-to-all-start.1 = ((f32[8,256,512]{1,2,0:T(8,128)}), f32[8,256,512]{1,2,0:T(8,128)}, u32[]{:S(2)}, u32[]{:S(2)}) async-start(f32[8,256,512]{1,2,0:T(8,128)} %stack.11), calls=%async_computation.1 | async-start | bytes 8388608 | tf_op jit(solution)/shard_map/all_to_all | solution.py:28
  112.7 0.3 all-gather.10.cloned.1.call-start
  113.0 0.1 copy.37
  113.1 0.1 broadcast_in_dim.70
  113.1 0.1 convert_element_type.94
  113.3 0.2 copy.38
  114.1 47.5 %all-to-all-done.1 = f32[8,256,512]{1,2,0:T(8,128)} async-done(((f32[8,256,512]{1,2,0:T(8,128)}), f32[8,256,512]{1,2,0:T(8,128)}, u32[]{:S(2)}, u32[]{:S(2)}) %all-to-all-start.1) | async-done | bytes 4194336 | tf_op jit(solution)/shard_map/all_to_all | solution.py:28
  161.6 12.7 %all-gather.8.cloned.1.call-done = f32[4096,512]{1,0:T(8,128)} async-done(((f32[256,512]{1,0:T(8,128)}), f32[4096,512]{1,0:T(8,128)}) %all-gather.8.cloned.1.call-update) | async-done | bytes 8388624 | tf_op jit(solution)/shard_map/all_gather | solution.py:35
  174.4 17.7 %fusion.1 = f32[256,512]{1,0:T(8,128)} fusion(f32[256,512]{1,0:T(8,128)S(1)} %copy.38, f32[256,512]{1,0:T(8,128)S(1)} %copy-done.4, pred[]{:T(512)} %bitcast.3, f32[256,4096]{0,1:T(8,128)} %bitcast.14, f32[4096,512]{1,0:T(8,128)} %all-gather.8.cloned.1.call-done), kind=kOutput, calls=%fused_computation.8 | convolution fusion | flops 6442975232 | bytes 14155777 | tf_op jit(solution)/shard_map/dot_general | solution.py:33
  192.1 1.2 copy.39
  193.3 2.3 stack.12
  195.6 5.3 %all-to-all-start.2 = ((f32[8,256,512]{1,2,0:T(8,128)}), f32[8,256,512]{1,2,0:T(8,128)}, u32[]{:S(2)}, u32[]{:S(2)}) async-start(f32[8,256,512]{1,2,0:T(8,128)} %stack.12), calls=%async_computation.2 | async-start | bytes 8388608 | tf_op jit(solution)/shard_map/all_to_all | solution.py:28
  200.9 0.5 all-gather.12.cloned.1.call-start
  201.4 0.1 copy.40
  201.6 0.1 convert_element_type.98
  201.7 0.2 copy.41
  202.6 47.2 %all-to-all-done.2 = f32[8,256,512]{1,2,0:T(8,128)} async-done(((f32[8,256,512]{1,2,0:T(8,128)}), f32[8,256,512]{1,2,0:T(8,128)}, u32[]{:S(2)}, u32[]{:S(2)}) %all-to-all-start.2) | async-done | bytes 4194336 | tf_op jit(solution)/shard_map/all_to_all | solution.py:28
  249.8 12.7 %all-gather.10.cloned.1.call-done = f32[4096,512]{1,0:T(8,128)} async-done(((f32[256,512]{1,0:T(8,128)}), f32[4096,512]{1,0:T(8,128)}) %all-gather.10.cloned.1.call-update) | async-done | bytes 8388624 | tf_op jit(solution)/shard_map/all_gather | solution.py:35
  262.6 17.7 %fusion.2 = f32[256,512]{1,0:T(8,128)} fusion(f32[256,512]{1,0:T(8,128)S(1)} %copy.41, f32[256,512]{1,0:T(8,128)S(1)} %copy-done.5, pred[]{:T(512)} %bitcast.2, f32[256,4096]{0,1:T(8,128)} %bitcast.18, f32[4096,512]{1,0:T(8,128)} %all-gather.10.cloned.1.call-done), kind=kOutput, calls=%fused_computation.9 | convolution fusion | flops 6442975232 | bytes 14155777 | tf_op jit(solution)/shard_map/dot_general | solution.py:33
  280.3 1.2 copy.42
  281.5 2.3 stack.13
  283.8 5.3 %all-to-all-start.3 = ((f32[8,256,512]{1,2,0:T(8,128)}), f32[8,256,512]{1,2,0:T(8,128)}, u32[]{:S(2)}, u32[]{:S(2)}) async-start(f32[8,256,512]{1,2,0:T(8,128)} %stack.13), calls=%async_computation.3 | async-start | bytes 8388608 | tf_op jit(solution)/shard_map/all_to_all | solution.py:28
  289.1 0.2 all-gather.14.cloned.1.call-start
  289.3 0.1 copy.43
  289.4 0.1 convert_element_type.102
  289.6 0.2 copy.44
  290.3 47.7 %all-to-all-done.3 = f32[8,256,512]{1,2,0:T(8,128)} async-done(((f32[8,256,512]{1,2,0:T(8,128)}), f32[8,256,512]{1,2,0:T(8,128)}, u32[]{:S(2)}, u32[]{:S(2)}) %all-to-all-start.3) | async-done | bytes 4194336 | tf_op jit(solution)/shard_map/all_to_all | solution.py:28
  338.0 12.7 %all-gather.12.cloned.1.call-done = f32[4096,512]{1,0:T(8,128)} async-done(((f32[256,512]{1,0:T(8,128)}), f32[4096,512]{1,0:T(8,128)}) %all-gather.12.cloned.1.call-update) | async-done | bytes 8388624 | tf_op jit(solution)/shard_map/all_gather | solution.py:35
  350.8 17.7 %fusion.3 = f32[256,512]{1,0:T(8,128)} fusion(f32[256,512]{1,0:T(8,128)S(1)} %copy.44, f32[256,512]{1,0:T(8,128)S(1)} %copy-done.6, pred[]{:T(512)} %bitcast.1, f32[256,4096]{0,1:T(8,128)} %bitcast.22, f32[4096,512]{1,0:T(8,128)} %all-gather.12.cloned.1.call-done), kind=kOutput, calls=%fused_computation.10 | convolution fusion | flops 6442975232 | bytes 14155777 | tf_op jit(solution)/shard_map/dot_general | solution.py:33
  368.5 1.2 copy.45
  369.7 2.3 stack.14
  372.0 5.5 %all-to-all-start.4 = ((f32[8,256,512]{1,2,0:T(8,128)}), f32[8,256,512]{1,2,0:T(8,128)}, u32[]{:S(2)}, u32[]{:S(2)}) async-start(f32[8,256,512]{1,2,0:T(8,128)} %stack.14), calls=%async_computation.4 | async-start | bytes 8388608 | tf_op jit(solution)/shard_map/all_to_all | solution.py:28
  377.6 0.1 copy.46
  377.7 0.1 convert_element_type.106
  377.9 0.2 copy.47
  378.7 47.8 %all-to-all-done.4 = f32[8,256,512]{1,2,0:T(8,128)} async-done(((f32[8,256,512]{1,2,0:T(8,128)}), f32[8,256,512]{1,2,0:T(8,128)}, u32[]{:S(2)}, u32[]{:S(2)}) %all-to-all-start.4) | async-done | bytes 4194336 | tf_op jit(solution)/shard_map/all_to_all | solution.py:28
  426.4 12.5 %all-gather.14.cloned.1.call-done = f32[4096,512]{1,0:T(8,128)} async-done(((f32[256,512]{1,0:T(8,128)}), f32[4096,512]{1,0:T(8,128)}) %all-gather.14.cloned.1.call-update) | async-done | bytes 8388624 | tf_op jit(solution)/shard_map/all_gather | solution.py:35
  439.0 17.7 %fusion.4 = f32[256,512]{1,0:T(8,128)} fusion(f32[256,512]{1,0:T(8,128)S(1)} %copy.47, f32[256,512]{1,0:T(8,128)S(1)} %copy-done.3, pred[]{:T(512)} %bitcast, f32[256,4096]{0,1:T(8,128)} %bitcast.26, f32[4096,512]{1,0:T(8,128)} %all-gather.14.cloned.1.call-done), kind=kOutput, calls=%fused_computation.11 | convolution fusion | flops 6442975232 | bytes 14155777 | tf_op jit(solution)/shard_map/dot_general | solution.py:33
  (35 shorter events, 0.6 us)
Async XLA Ops:
  6.5 0.9 copy-start
  6.5 79.6 %all-gather.6.cloned.1.call-start = ((), (), s32[]{:S(2)}) async-start(), calls=%async_computation.5 | async-start | bytes 8912896 | tf_op jit(solution)/shard_map/all_gather | solution.py:35
  15.7 7.4 %copy-start.7 = (s32[5]{0:T(128)S(1)}, s32[5]{0:T(128)}, u32[]{:S(2)}) copy-start(s32[5]{0:T(128)} %param.6) | copy-start | bytes 64
  15.7 70.4 %copy-start.2 = (f32[256,512]{1,0:T(8,128)S(1)}, f32[256,512]{1,0:T(8,128)}, u32[]{:S(2)}) copy-start(f32[256,512]{1,0:T(8,128)} %mul.45) | copy-start | bytes 1572868
  15.7 55.9 %all-to-all-start = ((f32[8,256,512]{1,2,0:T(8,128)}), f32[8,256,512]{1,2,0:T(8,128)}, u32[]{:S(2)}, u32[]{:S(2)}) async-start(f32[8,256,512]{1,2,0:T(8,128)} %stack.10), calls=%async_computation | async-start | bytes 8388608 | tf_op jit(solution)/shard_map/all_to_all | solution.py:28
  22.6 151.7 %all-gather.8.cloned.1.call-start = ((), (), s32[]{:S(2)}) async-start(), calls=%async_computation.6 | async-start | bytes 8912896 | tf_op jit(solution)/shard_map/all_gather | solution.py:35
  107.4 66.9 %copy-start.4 = (f32[256,512]{1,0:T(8,128)S(1)}, f32[256,512]{1,0:T(8,128)}, u32[]{:S(2)}) copy-start(f32[256,512]{1,0:T(8,128)} %fusion) | copy-start | bytes 1572868
  107.4 54.2 %all-to-all-start.1 = ((f32[8,256,512]{1,2,0:T(8,128)}), f32[8,256,512]{1,2,0:T(8,128)}, u32[]{:S(2)}, u32[]{:S(2)}) async-start(f32[8,256,512]{1,2,0:T(8,128)} %stack.11), calls=%async_computation.1 | async-start | bytes 8388608 | tf_op jit(solution)/shard_map/all_to_all | solution.py:28
  112.7 149.9 %all-gather.10.cloned.1.call-start = ((), (), s32[]{:S(2)}) async-start(), calls=%async_computation.7 | async-start | bytes 8912896 | tf_op jit(solution)/shard_map/all_gather | solution.py:35
  195.6 66.9 %copy-start.5 = (f32[256,512]{1,0:T(8,128)S(1)}, f32[256,512]{1,0:T(8,128)}, u32[]{:S(2)}) copy-start(f32[256,512]{1,0:T(8,128)} %fusion.1) | copy-start | bytes 1572868
  195.6 54.2 %all-to-all-start.2 = ((f32[8,256,512]{1,2,0:T(8,128)}), f32[8,256,512]{1,2,0:T(8,128)}, u32[]{:S(2)}, u32[]{:S(2)}) async-start(f32[8,256,512]{1,2,0:T(8,128)} %stack.12), calls=%async_computation.2 | async-start | bytes 8388608 | tf_op jit(solution)/shard_map/all_to_all | solution.py:28
  200.9 149.9 %all-gather.12.cloned.1.call-start = ((), (), s32[]{:S(2)}) async-start(), calls=%async_computation.8 | async-start | bytes 8912896 | tf_op jit(solution)/shard_map/all_gather | solution.py:35
  283.8 66.9 %copy-start.6 = (f32[256,512]{1,0:T(8,128)S(1)}, f32[256,512]{1,0:T(8,128)}, u32[]{:S(2)}) copy-start(f32[256,512]{1,0:T(8,128)} %fusion.2) | copy-start | bytes 1572868
  283.8 54.2 %all-to-all-start.3 = ((f32[8,256,512]{1,2,0:T(8,128)}), f32[8,256,512]{1,2,0:T(8,128)}, u32[]{:S(2)}, u32[]{:S(2)}) async-start(f32[8,256,512]{1,2,0:T(8,128)} %stack.13), calls=%async_computation.3 | async-start | bytes 8388608 | tf_op jit(solution)/shard_map/all_to_all | solution.py:28
  289.1 149.9 %all-gather.14.cloned.1.call-start = ((), (), s32[]{:S(2)}) async-start(), calls=%async_computation.9 | async-start | bytes 8912896 | tf_op jit(solution)/shard_map/all_gather | solution.py:35
  372.0 66.9 %copy-start.3 = (f32[256,512]{1,0:T(8,128)S(1)}, f32[256,512]{1,0:T(8,128)}, u32[]{:S(2)}) copy-start(f32[256,512]{1,0:T(8,128)} %fusion.3) | copy-start | bytes 1572868
  372.0 54.4 %all-to-all-start.4 = ((f32[8,256,512]{1,2,0:T(8,128)}), f32[8,256,512]{1,2,0:T(8,128)}, u32[]{:S(2)}, u32[]{:S(2)}) async-start(f32[8,256,512]{1,2,0:T(8,128)} %stack.14), calls=%async_computation.4 | async-start | bytes 8388608 | tf_op jit(solution)/shard_map/all_to_all | solution.py:28
  439.0 17.7 %copy-start.1 = (s32[6,64,64]{2,1,0:T(8,128)S(1)}, s32[6,64,64]{2,1,0:T(8,128)}, u32[]{:S(2)}) copy-start(s32[6,64,64]{2,1,0:T(8,128)} %param.5) | copy-start | bytes 294916
Sparse Core Ops, SparseCore 0:
  12.3 73.8 all-gather.5
  104.0 70.3 all-gather.7
  192.2 70.3 all-gather.9
  280.4 70.3 all-gather.11
  368.6 70.3 all-gather.13
